TPU v7x, 32 devices: a whole 2x2x4 slice. The times are simulated.
32 devices in a mesh: inputs: 8 (over z, y), tm: 4 (over x, core).
Axes of the slice: x: 2, y: 2, z: 4, core: 2. Of those that a mesh axis runs over, the one named last changes fastest.
Arguments:
- voltages: bfloat16 [128, 131072], P('inputs', 'tm'), may hold values from -8 to 8
- pfb_taps: float32 [8, 512], replicated, may hold values from -2 to 2
Outputs:
- visibilities: float32 [256, 1, 2, 128, 128], P(('inputs', 'tm'))
All inputs are finite; a program needn't handle non-finite values.
Results may differ from a plain program's by a relative error of at most 0.002.
Values may be sent and summed in bfloat16 or wider, within the bound.
No kernel may reach another device: no remote copies, remote signals or barrier semaphores. Data moves between devices by JAX's collectives and lax.ppermute only.
A program may use at most 128 MiB of HBM per device.

v0:
```python
import jax
import jax.numpy as jnp
from jax import lax
from jax.sharding import PartitionSpec as P

F = 256
TAPS = 8
TILE = 128
FRAME = 512


def from_behind(value, axis, steps):
    count = lax.axis_size(axis)
    initial, last = (max(0, -steps), min(count, count - steps))
    return lax.ppermute(value, axis, [(source, source + steps) for source in range(initial, last)])


def dft_table(chans, length):
    rows = jnp.arange(2 * chans, dtype=jnp.int32)
    freq = rows // 2
    part = rows % 2
    samp = jnp.arange(length, dtype=jnp.int32)
    phase = freq[:, None] * samp[None, :] % length
    angle = 2.0 * jnp.pi / length * phase.astype(jnp.float32)
    vals = jnp.where(part[:, None] == 0, jnp.cos(angle), -jnp.sin(angle))
    return (vals * (1.0 / length**0.5)).astype(jnp.bfloat16)


def tile_sums(spec, scale):
    left = jnp.concatenate([spec[:, 0], spec[:, 1]], axis=-1)
    twisted = jnp.concatenate([spec[:, 1], -spec[:, 0]], axis=-1)
    count_in = left.shape[1]
    blocks = count_in // TILE
    chans = left.shape[0]
    real_rows = []
    imag_rows = []
    for first in range(blocks):
        lower = first * TILE
        cols = left[:, lower:]
        real_part = jnp.einsum(
            "cik,cjk->cij", left[:, lower : lower + TILE], cols, preferred_element_type=jnp.float32
        )
        imag_part = jnp.einsum(
            "cik,cjk->cij",
            twisted[:, lower : lower + TILE],
            cols,
            preferred_element_type=jnp.float32,
        )
        count = blocks - first
        real_rows.append(real_part.reshape(chans, TILE, count, TILE).transpose(0, 2, 1, 3))
        imag_rows.append(imag_part.reshape(chans, TILE, count, TILE).transpose(0, 2, 1, 3))
    real_all = jnp.concatenate(real_rows, axis=1)
    imag_all = jnp.concatenate(imag_rows, axis=1)
    return jnp.stack([real_all, imag_all], axis=2) * scale


def on_device(voltages, pfb_taps):
    inp_local = voltages.shape[0]
    frames_local = voltages.shape[1] // FRAME
    previous = from_behind(voltages[:, voltages.shape[1] - (TAPS - 1) * FRAME :], "tm", 1)
    extended = jnp.concatenate([previous, voltages], axis=1).reshape(
        inp_local, frames_local + TAPS - 1, FRAME
    )
    filtered = jnp.zeros((inp_local, frames_local, FRAME), jnp.float32)
    for tap in range(TAPS):
        filtered = filtered + pfb_taps[tap][None, None, :] * extended[
            :, tap : tap + frames_local, :
        ].astype(jnp.float32)
    filtered = filtered.astype(jnp.bfloat16)
    table = dft_table(F, FRAME)
    spectra = jnp.einsum("kn,itn->kit", table, filtered, preferred_element_type=jnp.float32)
    spectra = spectra.astype(jnp.bfloat16).reshape(F, 2, inp_local, frames_local)
    blocks_time = lax.axis_size("tm")
    scale = 1.0 / (frames_local * blocks_time)
    turned = lax.all_to_all(
        lax.all_to_all(spectra, "inputs", split_axis=0, concat_axis=2, tiled=True),
        "tm",
        split_axis=0,
        concat_axis=3,
        tiled=True,
    )
    return tile_sums(turned, scale)


def solution(mesh):
    in_specs = (P("inputs", "tm"), P())
    out_specs = P(("inputs", "tm"), None, None, None, None)
    return jax.shard_map(
        on_device, mesh=mesh, in_specs=in_specs, out_specs=out_specs, check_vma=False
    )
```

profile of v0, /device:TPU:0, one launch (start us, length us, event | category | flops | bytes accessed | tf_op | source)
XLA Modules:
  0.0 76.3 jit_solution(17021184768935166234)
XLA Ops:
  0.0 0.9 %slice.60 = bf16[16,3584]{1,0:T(8,128)(2,1)S(1)} slice(bf16[16,32768]{1,0:T(8,128)(2,1)} %param.2), slice={[0:16], [29184:32768]} | slice | bytes 229376 | tf_op jit(solution)/shard_map/slice | solution.py:60
  0.9 2.4 %collective-permute-start = (bf16[16,3584]{1,0:T(8,128)(2,1)S(1)}, bf16[16,3584]{1,0:T(8,128)(2,1)S(1)}, u32[]{:S(2)}, u32[]{:S(2)}) collective-permute-start(bf16[16,3584]{1,0:T(8,128)(2,1)S(1)} %slice.60), channel_id=1, source_target_pairs={{0,1},{1,2},{2,3},{4,5},{5,6},{6,7},{8,9},{9,10},{10,11},{12,13},{... | collective-permute-start | bytes 344072 | tf_op jit(solution)/shard_map/ppermute | solution.py:15
  3.3 1.0 %fusion.32 = (f32[1,512]{1,0:T(1,128)S(1)}, f32[1,512]{1,0:T(1,128)S(1)}, f32[1,512]{1,0:T(1,128)S(1)}, f32[1,512]{1,0:T(1,128)S(1)}, f32[1,512]{1,0:T(1,128)S(1...) fusion(f32[8,512]{1,0:T(8,128)} %param.3), kind=kLoop, calls=%fused_computation.48 | loop fusion | bytes 32768 | tf_op jit(solution)/shard_map/slice | solution.py:66
  4.4 0.0 collective-permute-done
  4.4 1.3 %pad_maximum_fusion = bf16[16,36352]{1,0:T(8,128)(2,1)S(1)} fusion(bf16[16,32768]{1,0:T(8,128)(2,1)} %param.2, bf16[16,3584]{1,0:T(8,128)(2,1)S(1)} %collective-permute-done), kind=kLoop, calls=%fused_computation.7 | loop fusion | flops 2326528 | bytes 2326528 | tf_op jit(solution)/shard_map/concatenate | solution.py:61
  5.7 0.7 reshape.74
  6.4 6.5 %convolution_convert_fusion = bf16[512,16,64]{0,2,1:T(8,128)(2,1)S(1)} fusion(bf16[16,71,512]{2,1,0:T(8,128)(2,1)S(1)} %reshape.74, f32[512]{0:T(512)S(1)} %bitcast.42, f32[512]{0:T(512)S(1)} %bitcast.43, f32[512]{0:T(512)S(1)} %bitcast.37, f32[512]{0:T(512)S(1)} %bitcast.38, f32[512]{0:T(512)S(1)} %bitcast.39, f32[512]{0:T(512)S(1)} %bitcast.40, ...), kind=kOutput, calls=%fused_computation.4 | convolution fusion | flops 554696704 | bytes 9456128 | tf_op jit(solution)/shard_map/kn,itn->kit/dot_general | solution.py:71
  12.9 2.0 %copy.11 = bf16[512,16,64]{2,1,0:T(8,128)(2,1)S(1)} copy(bf16[512,16,64]{0,2,1:T(8,128)(2,1)S(1)} %convolution_convert_fusion) | data formatting | bytes 2097152 | tf_op jit(solution)/shard_map/convert_element_type | solution.py:72
  15.0 1.7 %reshape.77 = bf16[8,2,32768]{2,1,0:T(2,128)(2,1)S(1)} reshape(bf16[256,2,16,64]{3,2,1,0:T(8,128)(2,1)S(1)} %bitcast.27) | data formatting | bytes 2097152
  16.7 32.5 %all_to_all.36 = bf16[8,2,32768]{2,1,0:T(2,128)(2,1)} all-to-all(bf16[8,2,32768]{2,1,0:T(2,128)(2,1)S(1)} %reshape.77), channel_id=1, replica_groups=mesh['inputs'=8,'tm'=4] {'inputs'}, dimensions={0} | all-to-all | bytes 2097152 | tf_op jit(solution)/shard_map/all_to_all | solution.py:76
  49.1 3.1 %reshape.78 = bf16[256,2,16,64]{3,2,1,0:T(8,128)(2,1)S(1)} reshape(bf16[8,2,32768]{2,1,0:T(2,128)(2,1)} %all_to_all.36) | data formatting | bytes 2097152
  52.2 2.0 %copy.12 = bf16[8,32,2,16,64]{4,3,0,2,1:T(8,128)(2,1)} copy(bf16[8,32,2,16,64]{4,3,2,1,0:T(8,128)(2,1)S(1)} %bitcast.28) | data formatting | bytes 2097152 | tf_op jit(solution)/shard_map/all_to_all | solution.py:76
  54.2 2.0 %copy.13 = bf16[32,2,128,64]{2,3,1,0:T(8,128)(2,1)S(1)} copy(bf16[32,2,128,64]{3,2,1,0:T(8,128)(2,1)} %bitcast.29) | data formatting | bytes 2097152 | tf_op jit(solution)/shard_map/all_to_all | solution.py:76
  56.2 17.4 %all_to_all.37 = bf16[32,2,128,64]{2,3,1,0:T(8,128)(2,1)S(1)} all-to-all(bf16[32,2,128,64]{2,3,1,0:T(8,128)(2,1)S(1)} %copy.13), channel_id=1, replica_groups=mesh['inputs'=8,'tm'=4] {'tm'}, dimensions={0} | all-to-all | bytes 2097152 | tf_op jit(solution)/shard_map/all_to_all | solution.py:75
  73.6 0.1 copy.14
  73.7 0.1 fusion.31
  73.8 0.2 copy.19
  74.0 0.2 copy.18
  74.3 0.4 convolution_bitcast_fusion.1
  74.7 0.4 convolution_bitcast_fusion
  75.2 0.1 maximum_multiply_fusion
  75.3 1.1 %copy.17 = f32[8,1,2,128,128]{4,3,2,1,0:T(8,128)} copy(f32[8,1,2,128,128]{4,3,0,2,1:T(8,128)S(1)} %maximum_multiply_fusion) | data formatting | bytes 2097152 | tf_op jit(solution)/shard_map/mul | solution.py:54
  (3 shorter events, 0.0 us)
Async XLA Ops:
  0.9 3.5 %collective-permute-start = (bf16[16,3584]{1,0:T(8,128)(2,1)S(1)}, bf16[16,3584]{1,0:T(8,128)(2,1)S(1)}, u32[]{:S(2)}, u32[]{:S(2)}) collective-permute-start(bf16[16,3584]{1,0:T(8,128)(2,1)S(1)} %slice.60), channel_id=1, source_target_pairs={{0,1},{1,2},{2,3},{4,5},{5,6},{6,7},{8,9},{9,10},{10,11},{12,13},{... | collective-permute-start | bytes 344072 | tf_op jit(solution)/shard_map/ppermute | solution.py:15
where the time goes:
time: 76.7 us; the launch traced here: 76.3 us
  blocking collectives  49.9 us (65%)
  local copies, waits for them, and re-layouts  15.1 us (20%)
  matrix products  7.4 us (10%)
  starting transfers between devices  2.39 us (3%)
  other arithmetic  1.43 us (2%)
    all_to_all x1, blocking collectives, on_device(): lax.all_to_all(spectra, 'inputs', split_axis=0, concat_axis=2, tiled=True)  32.5 us
    all_to_all x1, blocking collectives, on_device(): lax.all_to_all(lax.all_to_all(spectra, 'inputs', split_axis=0, concat_axi...  17.4 us
    dot_general x1, matrix products, on_device(): jnp.einsum('kn,itn->kit', table, filtered, preferred_element_type=jnp.flo...  6.55 us
    unnamed x4, local copies, waits for them, and re-layouts  5.2 us
    all_to_all x2, local copies, waits for them, and re-layouts, on_device(): lax.all_to_all(spectra, 'inputs', split_axis=0, concat_axis=2, tiled=True)  3.96 us
    ppermute x1, starting transfers between devices, from_behind(): lax.ppermute(value, axis, [(source, source + steps) for source in range(i...  2.39 us
    convert_element_type x1, local copies, waits for them, and re-layouts, on_device(): spectra.astype(jnp.bfloat16).reshape(F, 2, inp_local, frames_local)  2.03 us
  transfers between devices with their start and end apart: 1, of which 0 were waited for; matrix products, arithmetic and copies ran while one was open for 1% of the time, Pallas kernels for 0%

commit v1 on v0

--- a/solution.py
+++ b/solution.py
@@ -73,7 +73,12 @@
     blocks_time = lax.axis_size("tm")
     scale = 1.0 / (frames_local * blocks_time)
     turned = lax.all_to_all(
-        lax.all_to_all(spectra, "inputs", split_axis=0, concat_axis=2, tiled=True),
+        jnp.concatenate(
+            lax.all_to_all(
+                jnp.stack(jnp.split(spectra, lax.axis_size("inputs"), axis=0)), "inputs", 0, 0
+            ),
+            axis=2,
+        ),
         "tm",
         split_axis=0,
         concat_axis=3,

time: 76.7 us -> 83.9 us (1.094)
  local copies, waits for them, and re-layouts: 15.1 us -> 22.2 us
    split x0 -> x9, local copies, waits for them, and re-layouts: none -> 6.7 us  [on_device(): jnp.split(spectra, lax.axis_size('inputs'), axis=0)]
    reshape x0 -> x2, local copies, waits for them, and re-layouts: none -> 3.96 us  [on_device(): jnp.concatenate(lax.all_to_all(jnp.stack(jnp.split(spectra, lax.axis_size...]
    all_to_all x3 -> x1, local copies, waits for them, and re-layouts: 4.05 us -> 0.09 us  [on_device(): lax.all_to_all(jnp.concatenate(lax.all_to_all(jnp.stack(jnp.split(spectra...]
    unnamed x4 -> x15, local copies, waits for them, and re-layouts: 5.2 us -> 7.57 us
    convert_element_type x1 -> x0, local copies, waits for them, and re-layouts: 2.03 us -> none  [on_device(): spectra.astype(jnp.bfloat16).reshape(F, 2, inp_local, frames_local)]
where the time goes in v1:
time: 83.9 us; the launch traced here: 83.4 us
  blocking collectives  49.8 us (59%)
  local copies, waits for them, and re-layouts  22.2 us (26%)
  matrix products  7.4 us (9%)
  starting transfers between devices  2.39 us (3%)
  other arithmetic  1.43 us (2%)
    all_to_all x1, blocking collectives, on_device(): lax.all_to_all(jnp.stack(jnp.split(spectra, lax.axis_size('inputs'), axis...  32.4 us
    all_to_all x1, blocking collectives, on_device(): lax.all_to_all(jnp.concatenate(lax.all_to_all(jnp.stack(jnp.split(spectra...  17.4 us
    unnamed x15, local copies, waits for them, and re-layouts  7.57 us
    split x9, local copies, waits for them, and re-layouts, on_device(): jnp.split(spectra, lax.axis_size('inputs'), axis=0)  6.7 us
    dot_general x1, matrix products, on_device(): jnp.einsum('kn,itn->kit', table, filtered, preferred_element_type=jnp.flo...  6.55 us
    reshape x2, local copies, waits for them, and re-layouts, on_device(): jnp.concatenate(lax.all_to_all(jnp.stack(jnp.split(spectra, lax.axis_size...  3.96 us
    ppermute x1, starting transfers between devices, from_behind(): lax.ppermute(value, axis, [(source, source + steps) for source in range(i...  2.39 us
  transfers between devices with their start and end apart: 1, of which 0 were waited for; matrix products, arithmetic and copies ran while one was open for 1% of the time, Pallas kernels for 0%

profile of v1, /device:TPU:0, one launch (start us, length us, event | category | flops | bytes accessed | tf_op | source)
XLA Modules:
  0.0 83.4 jit_solution(18238531320039831594)
XLA Ops:
  0.0 0.9 %slice.68 = bf16[16,3584]{1,0:T(8,128)(2,1)S(1)} slice(bf16[16,32768]{1,0:T(8,128)(2,1)} %param.2), slice={[0:16], [29184:32768]} | slice | bytes 229376 | tf_op jit(solution)/shard_map/slice | solution.py:60
  0.9 2.4 %collective-permute-start = (bf16[16,3584]{1,0:T(8,128)(2,1)S(1)}, bf16[16,3584]{1,0:T(8,128)(2,1)S(1)}, u32[]{:S(2)}, u32[]{:S(2)}) collective-permute-start(bf16[16,3584]{1,0:T(8,128)(2,1)S(1)} %slice.68), channel_id=1, source_target_pairs={{0,1},{1,2},{2,3},{4,5},{5,6},{6,7},{8,9},{9,10},{10,11},{12,13},{... | collective-permute-start | bytes 344072 | tf_op jit(solution)/shard_map/ppermute | solution.py:15
  3.3 1.0 %fusion.33 = (f32[1,512]{1,0:T(1,128)S(1)}, f32[1,512]{1,0:T(1,128)S(1)}, f32[1,512]{1,0:T(1,128)S(1)}, f32[1,512]{1,0:T(1,128)S(1)}, f32[1,512]{1,0:T(1,128)S(1...) fusion(f32[8,512]{1,0:T(8,128)} %param.3), kind=kLoop, calls=%fused_computation.57 | loop fusion | bytes 32768 | tf_op jit(solution)/shard_map/slice | solution.py:66
  4.4 1.3 %pad_maximum_fusion = bf16[16,36352]{1,0:T(8,128)(2,1)S(1)} fusion(bf16[16,32768]{1,0:T(8,128)(2,1)} %param.2, bf16[16,3584]{1,0:T(8,128)(2,1)S(1)} %collective-permute-done), kind=kLoop, calls=%fused_computation.7 | loop fusion | flops 2326528 | bytes 2326528 | tf_op jit(solution)/shard_map/concatenate | solution.py:61
  5.7 0.7 reshape.94
  6.4 6.5 %convolution_convert_fusion = bf16[512,16,64]{0,2,1:T(8,128)(2,1)S(1)} fusion(bf16[16,71,512]{2,1,0:T(8,128)(2,1)S(1)} %reshape.94, f32[512]{0:T(512)S(1)} %bitcast.54, f32[512]{0:T(512)S(1)} %bitcast.55, f32[512]{0:T(512)S(1)} %bitcast.49, f32[512]{0:T(512)S(1)} %bitcast.50, f32[512]{0:T(512)S(1)} %bitcast.51, f32[512]{0:T(512)S(1)} %bitcast.52, ...), kind=kOutput, calls=%fused_computation.4 | convolution fusion | flops 554696704 | bytes 9456128 | tf_op jit(solution)/shard_map/kn,itn->kit/dot_general | solution.py:71
  12.9 0.6 fusion.32
  13.8 0.9 %copy.36 = bf16[64,16,64]{2,1,0:T(8,128)(2,1)} copy(bf16[64,16,64]{0,2,1:T(8,128)(2,1)S(1)} %get-tuple-element.8) | data formatting | bytes 262144 | tf_op jit(solution)/shard_map/split | solution.py:78
  14.7 0.9 %copy.35 = bf16[64,16,64]{2,1,0:T(8,128)(2,1)} copy(bf16[64,16,64]{0,2,1:T(8,128)(2,1)S(1)} %get-tuple-element.9) | data formatting | bytes 262144 | tf_op jit(solution)/shard_map/split | solution.py:78
  15.9 0.9 %copy.33 = bf16[64,16,64]{2,1,0:T(8,128)(2,1)} copy(bf16[64,16,64]{0,2,1:T(8,128)(2,1)S(1)} %get-tuple-element.11) | data formatting | bytes 262144 | tf_op jit(solution)/shard_map/split | solution.py:78
  16.9 0.9 %copy.32 = bf16[64,16,64]{2,1,0:T(8,128)(2,1)} copy(bf16[64,16,64]{0,2,1:T(8,128)(2,1)S(1)} %get-tuple-element.12) | data formatting | bytes 262144 | tf_op jit(solution)/shard_map/split | solution.py:78
  17.8 0.9 %copy.31 = bf16[64,16,64]{2,1,0:T(8,128)(2,1)} copy(bf16[64,16,64]{0,2,1:T(8,128)(2,1)S(1)} %get-tuple-element.13) | data formatting | bytes 262144 | tf_op jit(solution)/shard_map/split | solution.py:78
  18.7 0.9 %copy.30 = bf16[64,16,64]{2,1,0:T(8,128)(2,1)} copy(bf16[64,16,64]{0,2,1:T(8,128)(2,1)S(1)} %get-tuple-element.14) | data formatting | bytes 262144 | tf_op jit(solution)/shard_map/split | solution.py:78
  19.7 1.0 %constant_dynamic-update-slice_fusion.7 = bf16[8,32,2,16,64]{4,3,2,1,0:T(8,128)(2,1)S(1)} fusion(bf16[1,32,2,16,64]{4,3,2,1,0:T(8,128)(2,1)} %bitcast.45), kind=kLoop, calls=%fused_computation.35 | loop fusion | bytes 393216
  20.6 1.0 %constant_dynamic-update-slice_fusion.6 = bf16[8,32,2,16,64]{4,3,2,1,0:T(8,128)(2,1)S(1)} fusion(bf16[8,32,2,16,64]{4,3,2,1,0:T(8,128)(2,1)S(1)} %constant_dynamic-update-slice_fusion.7, bf16[1,32,2,16,64]{4,3,2,1,0:T(8,128)(2,1)} %bitcast.44), kind=kLoop, calls=%fused_computation.34 | loop fusion | bytes 393216
  21.6 1.0 %constant_dynamic-update-slice_fusion.5 = bf16[8,32,2,16,64]{4,3,2,1,0:T(8,128)(2,1)S(1)} fusion(bf16[8,32,2,16,64]{4,3,2,1,0:T(8,128)(2,1)S(1)} %constant_dynamic-update-slice_fusion.6, bf16[1,32,2,16,64]{4,3,2,1,0:T(8,128)(2,1)} %bitcast.43), kind=kLoop, calls=%fused_computation.33 | loop fusion | bytes 393216
  22.6 1.0 %constant_dynamic-update-slice_fusion.4 = bf16[8,32,2,16,64]{4,3,2,1,0:T(8,128)(2,1)S(1)} fusion(bf16[8,32,2,16,64]{4,3,2,1,0:T(8,128)(2,1)S(1)} %constant_dynamic-update-slice_fusion.5, bf16[1,32,2,16,64]{4,3,2,1,0:T(8,128)(2,1)} %bitcast.42), kind=kLoop, calls=%fused_computation.32 | loop fusion | bytes 393216
  23.8 1.7 %reshape.98 = bf16[8,2,32768]{2,1,0:T(2,128)(2,1)S(1)} reshape(bf16[8,32,2,16,64]{4,3,2,1,0:T(8,128)(2,1)S(1)} %constant_dynamic-update-slice_fusion) | data formatting | bytes 2097152
  25.5 32.4 %all_to_all.23 = bf16[8,2,32768]{2,1,0:T(2,128)(2,1)S(1)} all-to-all(bf16[8,2,32768]{2,1,0:T(2,128)(2,1)S(1)} %reshape.98), channel_id=1, replica_groups=mesh['inputs'=8,'tm'=4] {'inputs'}, dimensions={0} | all-to-all | bytes 2097152 | tf_op jit(solution)/shard_map/all_to_all | solution.py:77
  57.8 1.4 %reshape.99 = bf16[8,32,2,16,64]{4,3,2,1,0:T(8,128)(2,1)S(1)} reshape(bf16[8,2,32768]{2,1,0:T(2,128)(2,1)S(1)} %all_to_all.23) | data formatting | bytes 2097152
  59.3 2.0 %copy.38 = bf16[32,2,8,16,64]{4,3,2,1,0:T(8,128)(2,1)} copy(bf16[32,2,8,16,64]{4,3,1,0,2:T(8,128)(2,1)S(1)} %bitcast.32) | data formatting | bytes 2097152 | tf_op jit(solution)/shard_map/reshape | solution.py:76
  61.2 2.0 %copy.39 = bf16[32,2,128,64]{2,3,1,0:T(8,128)(2,1)S(1)} copy(bf16[32,2,128,64]{3,2,1,0:T(8,128)(2,1)} %bitcast.33) | data formatting | bytes 2097152 | tf_op jit(solution)/shard_map/reshape | solution.py:76
  63.2 17.4 %all_to_all.24 = bf16[32,2,128,64]{2,3,1,0:T(8,128)(2,1)S(1)} all-to-all(bf16[32,2,128,64]{2,3,1,0:T(8,128)(2,1)S(1)} %copy.39), channel_id=1, replica_groups=mesh['inputs'=8,'tm'=4] {'tm'}, dimensions={0} | all-to-all | bytes 2097152 | tf_op jit(solution)/shard_map/all_to_all | solution.py:75
  82.3 1.1 %copy.43 = f32[8,1,2,128,128]{4,3,2,1,0:T(8,128)} copy(f32[8,1,2,128,128]{4,3,0,2,1:T(8,128)S(1)} %maximum_multiply_fusion) | data formatting | bytes 2097152 | tf_op jit(solution)/shard_map/mul | solution.py:54
  (21 shorter events, 2.3 us)
Async XLA Ops:
  0.9 3.5 %collective-permute-start = (bf16[16,3584]{1,0:T(8,128)(2,1)S(1)}, bf16[16,3584]{1,0:T(8,128)(2,1)S(1)}, u32[]{:S(2)}, u32[]{:S(2)}) collective-permute-start(bf16[16,3584]{1,0:T(8,128)(2,1)S(1)} %slice.68), channel_id=1, source_target_pairs={{0,1},{1,2},{2,3},{4,5},{5,6},{6,7},{8,9},{9,10},{10,11},{12,13},{... | collective-permute-start | bytes 344072 | tf_op jit(solution)/shard_map/ppermute | solution.py:15
  16.9 6.8 %copy-start.1 = (bf16[64,16,64]{2,1,0:T(8,128)(2,1)S(1)}, bf16[64,16,64]{2,1,0:T(8,128)(2,1)}, u32[]{:S(2)}) copy-start(bf16[64,16,64]{2,1,0:T(8,128)(2,1)} %copy.35) | copy-start | bytes 393220
  17.8 5.9 %copy-start = (bf16[64,16,64]{2,1,0:T(8,128)(2,1)S(1)}, bf16[64,16,64]{2,1,0:T(8,128)(2,1)}, u32[]{:S(2)}) copy-start(bf16[64,16,64]{2,1,0:T(8,128)(2,1)} %copy.36) | copy-start | bytes 393220
